TPU v7x, 512 devices: a whole 4x8x8 slice. The times are simulated.
512 devices in a mesh: dp: 4 (over y_hi), seq: 128 (over y_lo, x, z, core).
Axes of the slice: x: 4, y: 8 (y_hi: 4, y_lo: 2; y = y_hi * 2 + y_lo), z: 8, core: 2. Of those that a mesh axis runs over, the one named last changes fastest.
Arguments:
- queries: bfloat16 [4, 16384, 512], P('dp', 'seq'), may hold values from -6 to 6
- key_rows: bfloat16 [4, 16384, 512], P('dp', 'seq'), may hold values from -6 to 6
- value_rows: bfloat16 [4, 16384, 512], P('dp', 'seq'), may hold values from -6 to 6
- out_grad: bfloat16 [4, 16384, 1024], P('dp', 'seq'), may hold values from -6 to 6
- out_weight: bfloat16 [512, 1024], P('seq'), may hold values from -0.25 to 0.25
- norm_gain: float32 [256], replicated, may hold values from 0.1 to 1.9
Outputs:
- query_grad: bfloat16 [4, 16384, 512], P('dp', 'seq')
- key_grad: bfloat16 [4, 16384, 512], P('dp', 'seq')
- value_grad: bfloat16 [4, 16384, 512], P('dp', 'seq')
- weight_grad: float32 [512, 1024], P('seq')
All inputs are finite; a program needn't handle non-finite values.
Results may differ from a plain program's by a relative error of at most 0.025.
Values may be sent and summed in bfloat16 or wider, within the bound.
A program may use at most 64 MiB of HBM per device.

v0:
```python
import math
import jax
import jax.numpy as jnp
from jax import lax
from jax.sharding import PartitionSpec as P

DH = 128
SOFT_HEADS = 2
LIN_HEADS = 2
WINDOW = 256
HALF = 128
norm_eps = 1e-06


def with_halo(block, sides, width):
    for axis, dim in sides:
        count = lax.axis_size(axis)
        forward = [(i, i + 1) for i in range(count - 1)]
        forward.append((count - 1, 0))
        backward = [(target, source) for source, target in forward]
        low = lax.ppermute(
            lax.slice_in_dim(block, block.shape[dim] - width, None, axis=dim), axis, forward
        )
        high = lax.ppermute(lax.slice_in_dim(block, 0, width, axis=dim), axis, backward)
        block = jnp.concatenate([low, block, high], axis=dim)
    return block


def from_behind(value, axis, steps):
    count = lax.axis_size(axis)
    pairs = [(source, (source + steps) % count) for source in range(count)]
    return lax.ppermute(value, axis, pairs)


def unit_plus(values):
    return jnp.where(values > 0, values + 1.0, jnp.exp(jnp.minimum(values, 0.0)))


def unit_slope(values):
    return jnp.where(values > 0, 1.0, jnp.exp(jnp.minimum(values, 0.0)))


def body(queries, key_rows, value_rows, out_grad, out_weight, norm_gain):
    highest = lax.Precision.HIGHEST
    query_all = queries[0]
    key_all = key_rows[0]
    value_all = value_rows[0]
    grad_out = out_grad[0]
    tok_rows = query_all.shape[0]
    soft = SOFT_HEADS * DH
    factor = DH ** (-0.5)
    span_rows = tok_rows + 2 * HALF
    key_value = jnp.stack([key_all[:, :soft], value_all[:, :soft]])
    padded = with_halo(key_value, (("seq", 1),), HALF)
    query_soft = query_all[:, :soft].reshape(tok_rows, SOFT_HEADS, DH)
    key_soft = padded[0].reshape(span_rows, SOFT_HEADS, DH)
    value_soft = padded[1].reshape(span_rows, SOFT_HEADS, DH)
    scores = (
        jnp.einsum("ihd,jhd->hij", query_soft, key_soft, preferred_element_type=jnp.float32)
        * factor
    )
    row_pos = lax.broadcasted_iota(jnp.int32, (tok_rows, span_rows), 0)
    col_pos = lax.broadcasted_iota(jnp.int32, (tok_rows, span_rows), 1)
    inside = (col_pos >= row_pos) & (col_pos < row_pos + WINDOW)
    scores = jnp.where(inside, scores, -1e30)
    row_peak = jnp.max(scores, axis=2, keepdims=True)
    exp_terms = jnp.where(inside, jnp.exp(scores - row_peak), 0.0)
    attn_probs = exp_terms / jnp.sum(exp_terms, axis=2, keepdims=True)
    probs_low = attn_probs.astype(jnp.bfloat16)
    attn_soft = jnp.einsum(
        "hij,jhd->ihd", probs_low, value_soft, preferred_element_type=jnp.float32
    ).astype(jnp.bfloat16)
    query_lin = query_all[:, soft:].astype(jnp.float32).reshape(tok_rows, LIN_HEADS, DH)
    key_lin = key_all[:, soft:].astype(jnp.float32).reshape(tok_rows, LIN_HEADS, DH)
    value_lin = value_all[:, soft:].astype(jnp.float32).reshape(tok_rows, LIN_HEADS, DH)
    phi_query = unit_plus(query_lin)
    phi_key = unit_plus(key_lin)
    state_term = jnp.einsum("jha,jhb->hab", phi_key, value_lin, precision=highest)
    lin_state = lax.psum(state_term, "seq")
    lin_u = jnp.einsum("iha,hab->ihb", phi_query, lin_state, precision=highest)
    lin_r = lax.rsqrt(jnp.mean(lin_u * lin_u, axis=2, keepdims=True) + norm_eps)
    gain_heads = norm_gain.reshape(LIN_HEADS, DH)
    attn_lin = (gain_heads * lin_u * lin_r).astype(jnp.bfloat16)
    attn = jnp.concatenate(
        [attn_soft.reshape(tok_rows, soft), attn_lin.reshape(tok_rows, LIN_HEADS * DH)], axis=1
    )
    d_attn = lax.dot_general(
        grad_out,
        lax.all_gather(out_weight, "seq", axis=0, tiled=True),
        (((1,), (1,)), ((), ())),
        preferred_element_type=jnp.float32,
    ).astype(jnp.bfloat16)
    n_seq = lax.axis_size("seq")
    n_plasmid = lax.axis_size("dp")
    token_total = n_plasmid * n_seq * tok_rows
    local_term = lax.psum_scatter(
        lax.dot_general(
            attn, grad_out, (((0,), (0,)), ((), ())), preferred_element_type=jnp.float32
        ),
        "seq",
        scatter_dimension=0,
        tiled=True,
    )
    summed = lax.psum(local_term, "dp")
    weight_grad = summed * (1.0 / math.sqrt(token_total))
    dattn_soft = d_attn[:, :soft].reshape(tok_rows, SOFT_HEADS, DH)
    dprob = jnp.einsum("ihd,jhd->hij", dattn_soft, value_soft, preferred_element_type=jnp.float32)
    row_delta = jnp.sum(dattn_soft.astype(jnp.float32) * attn_soft.astype(jnp.float32), axis=2)
    dscore = (attn_probs * (dprob - row_delta.T[:, :, None])).astype(jnp.bfloat16)
    dq_soft = (
        jnp.einsum("hij,jhd->ihd", dscore, key_soft, preferred_element_type=jnp.float32) * factor
    )
    dk_span = (
        jnp.einsum("hij,ihd->jhd", dscore, query_soft, preferred_element_type=jnp.float32) * factor
    )
    dv_span = jnp.einsum("hij,ihd->jhd", probs_low, dattn_soft, preferred_element_type=jnp.float32)
    span_grads = jnp.stack([dk_span, dv_span]).reshape(2, span_rows, soft)
    from_next = from_behind(span_grads[:, :HALF], "seq", -1)
    from_prev = from_behind(span_grads[:, tok_rows + HALF :], "seq", 1)
    middle = span_grads[:, HALF : HALF + tok_rows]
    middle = middle + from_prev
    middle = middle + from_next
    lin_grad = gain_heads * d_attn[:, soft:].astype(jnp.float32).reshape(tok_rows, LIN_HEADS, DH)
    grad_u = lin_r * lin_grad - lin_u * lin_r**3 * jnp.mean(lin_grad * lin_u, axis=2, keepdims=True)
    dstate_term = jnp.einsum("iha,ihb->hab", phi_query, grad_u, precision=highest)
    dstate = lax.psum(dstate_term, "seq")
    dq_lin = jnp.einsum("ihb,hab->iha", grad_u, lin_state, precision=highest) * unit_slope(
        query_lin
    )
    dk_lin = jnp.einsum("jhb,hab->jha", value_lin, dstate, precision=highest) * unit_slope(key_lin)
    dv_lin = jnp.einsum("jha,hab->jhb", phi_key, dstate, precision=highest)
    lin_width = LIN_HEADS * DH
    query_grad = jnp.concatenate(
        [dq_soft.reshape(tok_rows, soft), dq_lin.reshape(tok_rows, lin_width)], axis=1
    ).astype(jnp.bfloat16)
    key_grad = jnp.concatenate([middle[0], dk_lin.reshape(tok_rows, lin_width)], axis=1).astype(
        jnp.bfloat16
    )
    value_grad = jnp.concatenate([middle[1], dv_lin.reshape(tok_rows, lin_width)], axis=1).astype(
        jnp.bfloat16
    )
    return (query_grad[None], key_grad[None], value_grad[None], weight_grad)


def solution(mesh):
    return jax.shard_map(
        body,
        mesh=mesh,
        in_specs=(
            P("dp", "seq", None),
            P("dp", "seq", None),
            P("dp", "seq", None),
            P("dp", "seq", None),
            P("seq", None),
            P(),
        ),
        out_specs=(
            P("dp", "seq", None),
            P("dp", "seq", None),
            P("dp", "seq", None),
            P("seq", None),
        ),
        check_vma=False,
    )
```

profile of v0, /device:TPU:8, one launch (start us, length us, event | category | flops | bytes accessed | tf_op | source)
XLA Modules:
  0.0 2277.1 jit_solution(10162035164895397284)
XLA Ops:
  8.0 1.0 copy.67
  9.0 1.0 copy.68
  10.1 12.5 collective-permute-start.1
  22.6 1.9 collective-permute-start
  24.5 0.9 fusion.45
  25.5 1.0 copy.69
  26.7 6.4 collective-permute-done
  33.5 196.6 %all-gather.3.cloned.1.call-done = bf16[128,4,1024]{2,1,0:T(4,128)(2,1)} async-done(((bf16[1,4,1024]{2,1,0:T(4,128)(2,1)}), bf16[128,4,1024]{2,1,0:T(4,128)(2,1)}) %all-gather.3.cloned.1.call-update) | async-done | bytes 1048592 | tf_op jit(solution)/shard_map/all_gather | solution.py:89
  230.1 1.3 reshape.183
  232.2 952.7 %all-reduce.5.cloned.1.call-done = f32[2,128,128]{2,1,0:T(8,128)} async-done(((f32[2,128,128]{2,1,0:T(8,128)}), f32[2,128,128]{2,1,0:T(8,128)}) %all-reduce.5.cloned.1.call-update) | async-done | bytes 131088 | tf_op jit(solution)/shard_map/psum | solution.py:79
  1184.9 1.3 multiply_reduce_fusion.1
  1186.9 1.7 fusion.19
  1188.6 1.1 fusion.33
  1189.8 1.3 dynamic-slice
  1193.4 1.9 collective-permute-start.2
  1195.3 7.9 collective-permute-start.3
  1204.2 1.3 collective-permute-done.2
  1205.5 1.8 collective-permute-done.3
  1207.3 1038.3 %all-reduce.7.cloned.1.call-done = (f32[2,128,128]{2,1,0:T(8,128)}, f32[512,1024]{1,0:T(8,128)}) async-done(((f32[2,128,128]{2,1,0:T(8,128)}, f32[512,1024]{1,0:T(8,128)}), (f32[2,128,128]{2,1,0:T(8,128)}, f32[512,1024]{1,0:T(8,128)})) %all-reduce.7.cloned.1.call-update) | async-done | bytes 2228240 | tf_op jit(solution)/shard_map/psum | solution.py:126
  2245.6 1.3 convolution_convert_fusion.2
  2246.9 1.1 fusion.13
  2248.0 0.8 constant_dynamic-slice_fusion
  2248.8 19.6 psum.23
  2269.1 0.8 copy.95
  (47 shorter events, 7.0 us)
Async XLA Ops:
  7.2 224.3 %copy-start = (bf16[1,128,1024]{2,1,0:T(8,128)(2,1)S(1)}, bf16[1,128,1024]{2,1,0:T(8,128)(2,1)}, u32[]{:S(2)}) copy-start(bf16[1,128,1024]{2,1,0:T(8,128)(2,1)} %param.9) | copy-start | bytes 786436
  7.2 222.9 %all-gather.3.cloned.1.call-start = ((), (), s32[]{:S(2)}) async-start(), calls=%async_computation.1 | async-start | bytes 1056768 | tf_op jit(solution)/shard_map/all_gather | solution.py:89
  7.9 1177.0 %all-reduce.5.cloned.1.call-start = ((), (), s32[]{:S(2)}) async-start(), calls=%async_computation | async-start | bytes 262144 | tf_op jit(solution)/shard_map/psum | solution.py:79
  10.1 16.6 collective-permute-start.1
  22.6 10.5 collective-permute-start
  25.5 2220.1 %all-reduce.7.cloned.1.call-start = ((), (), s32[]{:S(2)}) async-start(), calls=%async_computation.2 | async-start | bytes 4456448 | tf_op jit(solution)/shard_map/psum | solution.py:126
  33.5 1151.3 %copy-start.2 = (f32[256]{0:T(256)S(1)}, f32[256]{0:T(256)}, u32[]{:S(2)}) copy-start(f32[256]{0:T(256)} %param.11) | copy-start | bytes 3076
  1186.9 4.8 copy-start.1
  1193.4 12.0 collective-permute-start.2
  1195.3 11.9 collective-permute-start.3
Sparse Core Ops, SparseCore 0:
  10.1 219.9 all-gather.2
  233.6 951.2 all-reduce.4
  1189.9 1055.7 all-reduce.6
where the time goes:
time: 2280 us
  waiting for transfers between devices  2200 us (96%)
  starting transfers between devices  24.3 us (1%)
    psum x1, waiting for transfers between devices, body(): dstate = lax.psum(dstate_term, 'seq')  1040 us
    psum x1, waiting for transfers between devices, body(): lin_state = lax.psum(state_term, 'seq')  953 us
    all_gather x1, waiting for transfers between devices, body(): lax.all_gather(out_weight, 'seq', axis=0, tiled=True)  197 us
  transfers between devices with their start and end apart: 7, of which 6 were waited for; matrix products, arithmetic and copies ran while one was open for 0% of the time, Pallas kernels for 0%

commit v1 on v0

--- a/solution.py
+++ b/solution.py
@@ -123,7 +123,8 @@
     lin_grad = gain_heads * d_attn[:, soft:].astype(jnp.float32).reshape(tok_rows, LIN_HEADS, DH)
     grad_u = lin_r * lin_grad - lin_u * lin_r**3 * jnp.mean(lin_grad * lin_u, axis=2, keepdims=True)
     dstate_term = jnp.einsum("iha,ihb->hab", phi_query, grad_u, precision=highest)
-    dstate = lax.psum(dstate_term, "seq")
+    pieces = lax.all_gather(dstate_term, "seq")
+    dstate = jnp.sum(pieces, axis=0)
     dq_lin = jnp.einsum("ihb,hab->iha", grad_u, lin_state, precision=highest) * unit_slope(
         query_lin
     )

time: 2280 us -> 2530 us (1.11)
  the two profiles are of different devices: /device:TPU:8 before, /device:TPU:1 now
where the time goes in v1:
time: 2530 us
  waiting for transfers between devices  2460 us (97%)
    unnamed x5, waiting for transfers between devices  1090 us
    psum x1, waiting for transfers between devices, body(): lin_state = lax.psum(state_term, 'seq')  950 us
    all_gather x1, waiting for transfers between devices, body(): pieces = lax.all_gather(dstate_term, 'seq')  215 us
    all_gather x1, waiting for transfers between devices, body(): lax.all_gather(out_weight, 'seq', axis=0, tiled=True)  204 us
  transfers between devices with their start and end apart: 8, of which 6 were waited for; matrix products, arithmetic and copies ran while one was open for 1% of the time, Pallas kernels for 0%

profile of v1, /device:TPU:1, one launch (start us, length us, event | category | flops | bytes accessed | tf_op | source)
XLA Modules:
  0.0 2533.7 jit_solution(16657235458556284478)
XLA Ops:
  8.0 1.0 copy.67
  9.0 1.0 copy.68
  10.1 8.7 collective-permute-start.1
  18.8 1.9 collective-permute-start
  20.8 0.9 fusion.45
  21.8 1.0 copy.69
  23.0 4.9 collective-permute-done
  28.4 203.8 %all-gather.7.cloned.1.call-done = bf16[128,4,1024]{2,1,0:T(4,128)(2,1)} async-done(((bf16[1,4,1024]{2,1,0:T(4,128)(2,1)}), bf16[128,4,1024]{2,1,0:T(4,128)(2,1)}) %all-gather.7.cloned.1.call-update) | async-done | bytes 1048592 | tf_op jit(solution)/shard_map/all_gather | solution.py:89
  232.2 1.3 reshape.184
  234.2 950.0 %all-reduce.4.cloned.1.call-done = f32[2,128,128]{2,1,0:T(8,128)} async-done(((f32[2,128,128]{2,1,0:T(8,128)}), f32[2,128,128]{2,1,0:T(8,128)}) %all-reduce.4.cloned.1.call-update) | async-done | bytes 131088 | tf_op jit(solution)/shard_map/psum | solution.py:79
  1184.2 1.3 multiply_reduce_fusion.1
  1186.2 1.7 fusion.19
  1188.0 1.1 fusion.33
  1189.1 1.3 dynamic-slice
  1192.8 1.9 collective-permute-start.2
  1194.7 3.6 collective-permute-start.3
  1199.3 3.3 collective-permute-done.3
  1202.7 1084.5 %all-reduce.6.cloned.1.call-done = f32[512,1024]{1,0:T(8,128)} async-done(((f32[512,1024]{1,0:T(8,128)}), f32[512,1024]{1,0:T(8,128)}) %all-reduce.6.cloned.1.call-update) | async-done | bytes 2097168
  2287.2 0.8 constant_dynamic-slice_fusion
  2287.9 15.0 psum.15
  2303.6 214.8 %all-gather.5.cloned.1.call-done = f32[256,128,128]{2,1,0:T(8,128)} async-done(((f32[2,128,128]{2,1,0:T(8,128)}), f32[256,128,128]{2,1,0:T(8,128)}) %all-gather.5.cloned.1.call-update) | async-done | bytes 16777232 | tf_op jit(solution)/shard_map/all_gather | solution.py:126
  2518.4 6.6 reduce_sum.49
  2525.6 0.8 copy.95
  2526.4 0.8 copy.94
  (51 shorter events, 6.8 us)
Async XLA Ops:
  7.2 226.3 %copy-start = (bf16[1,128,1024]{2,1,0:T(8,128)(2,1)S(1)}, bf16[1,128,1024]{2,1,0:T(8,128)(2,1)}, u32[]{:S(2)}) copy-start(bf16[1,128,1024]{2,1,0:T(8,128)(2,1)} %param.9) | copy-start | bytes 786436
  7.2 225.0 %all-gather.7.cloned.1.call-start = ((), (), s32[]{:S(2)}) async-start(), calls=%async_computation.2 | async-start | bytes 1056768 | tf_op jit(solution)/shard_map/all_gather | solution.py:89
  7.9 1176.3 %all-reduce.4.cloned.1.call-start = ((), (), s32[]{:S(2)}) async-start(), calls=%async_computation | async-start | bytes 262144 | tf_op jit(solution)/shard_map/psum | solution.py:79
  10.1 12.9 collective-permute-start.1
  18.8 9.1 collective-permute-start
  21.8 2265.4 %all-reduce.6.cloned.1.call-start = ((), (), s32[]{:S(2)}) async-start(), calls=%async_computation.3 | async-start | bytes 4194304
  28.4 1155.8 %copy-start.2 = (f32[256]{0:T(256)S(1)}, f32[256]{0:T(256)}, u32[]{:S(2)}) copy-start(f32[256]{0:T(256)} %param.11) | copy-start | bytes 3076
  1186.2 4.9 copy-start.1
  1187.9 1330.5 %all-gather.5.cloned.1.call-start = ((), (), s32[]{:S(2)}) async-start(), calls=%async_computation.1 | async-start | bytes 16908288 | tf_op jit(solution)/shard_map/all_gather | solution.py:126
  1192.8 6.5 collective-permute-start.2
  1194.7 7.9 collective-permute-start.3
Sparse Core Ops, SparseCore 0:
  10.1 221.9 all-gather.6
  235.6 948.5 all-reduce.3
  1188.1 1099.0 all-reduce.5
  2289.8 228.5 all-gather.4
